TPU v7x, 32 devices: a whole 2x2x4 slice. The times are simulated.
32 devices in a mesh: chan: 8 (over z, y), facet: 4 (over x, core).
Axes of the slice: x: 2, y: 2, z: 4, core: 2. Of those that a mesh axis runs over, the one named last changes fastest.
Arguments:
- solution: float32 [8, 2048, 2048], P('chan', 'facet'), may hold values from -6 to 6
- residual: float32 [8, 2048, 2048], P('chan', 'facet'), may hold values from -120 to 120
- direction: float32 [8, 2048, 2048], P('chan', 'facet'), may hold values from -120 to 120
- spectra: float32 [8, 4096, 4096], P('chan', None, 'facet'), may hold values from 0.05 to 1
- basis: float32 [8, 8], replicated, may hold values from -2 to 2
- slot_channel: int32 [8], replicated, may hold values from 0 to 7, each once
Outputs:
- new_solution: float32 [8, 2048, 2048], P('chan', 'facet')
- new_residual: float32 [8, 2048, 2048], P('chan', 'facet')
- new_direction: float32 [8, 2048, 2048], P('chan', 'facet')
Inputs may be any that keep to these rules, and one draw needn't show every extreme that they name: `slot_channel`: every channel appears in exactly one slot.
All inputs are finite; a program needn't handle non-finite values.
Results may differ from a plain program's by a relative error of at most 0.000064.
Values sent between devices are 32-bit elements; how exact they have to be, the bound alone decides.
A program may use at most 256 MiB of HBM per device.

v0:
```python
import math
import jax
import jax.numpy as jnp
from jax import lax
from jax.sharding import PartitionSpec as P

ROOT = 64
HIGHEST = lax.Precision.HIGHEST
PRIOR_FLOOR = 0.25


def twiddle_table(left_size, right_size, length, direction_sign):
    product = (
        jnp.arange(left_size, dtype=jnp.int32)[:, None]
        * jnp.arange(right_size, dtype=jnp.int32)[None, :]
        % length
    )
    angles = product.astype(jnp.float32) * (2.0 * math.pi / length)
    return (jnp.cos(angles), direction_sign * jnp.sin(angles))


def complex_table(left_size, right_size, length, direction_sign):
    table_real, table_imag = twiddle_table(left_size, right_size, length, direction_sign)
    return jnp.stack([jnp.stack([table_real, table_imag]), jnp.stack([-table_imag, table_real])])


def real_table(left_size, right_size, length, direction_sign):
    table_real, table_imag = twiddle_table(left_size, right_size, length, direction_sign)
    return jnp.stack([table_real, table_imag])


def twisted(stacked, factor, direction_sign):
    table_real, table_imag = twiddle_table(factor, factor, factor * factor, direction_sign)
    table_real = table_real[:, :, None]
    table_imag = table_imag[:, :, None]
    real_in, imag_in = (stacked[0], stacked[1])
    return jnp.stack(
        [real_in * table_real - imag_in * table_imag, real_in * table_imag + imag_in * table_real]
    )


def forward_columns(planes, factor):
    halved = factor // 2
    groups, height = (planes.shape[0], planes.shape[1])
    blocks = planes.reshape(groups, height, halved, factor)
    section_one = jnp.einsum(
        "grjn,qjk->qgknr", blocks, real_table(halved, factor, factor, -1.0), precision=HIGHEST
    )
    section_one = twisted(section_one, factor, -1.0)
    second = jnp.einsum(
        "pgknr,pqnj->qgjkr",
        section_one,
        complex_table(factor, factor, factor, -1.0),
        precision=HIGHEST,
    )
    return second.reshape(2, groups, factor * factor, height)


def forward_rows(stacked, factor):
    halved = factor // 2
    groups, width = (stacked.shape[1], stacked.shape[2])
    blocks = stacked.reshape(2, groups, width, halved, factor)
    section_one = jnp.einsum(
        "pgcjn,pqjk->qgknc", blocks, complex_table(halved, factor, factor, -1.0), precision=HIGHEST
    )
    section_one = twisted(section_one, factor, -1.0)
    second = jnp.einsum(
        "pgknc,pqnj->qgjkc",
        section_one,
        complex_table(factor, factor, factor, -1.0),
        precision=HIGHEST,
    )
    return second.reshape(2, groups, factor * factor, width)


def inverse_rows(stacked, factor):
    halved = factor // 2
    groups, width = (stacked.shape[1], stacked.shape[3])
    blocks = stacked.reshape(2, groups, factor, factor, width)
    section_one = jnp.einsum(
        "pgjkc,pqjn->qgnkc", blocks, complex_table(factor, factor, factor, 1.0), precision=HIGHEST
    )
    section_one = twisted(section_one, factor, 1.0)
    second = jnp.einsum(
        "pgnkc,pqkj->qgjnc",
        section_one,
        complex_table(factor, halved, factor, 1.0),
        precision=HIGHEST,
    )
    return second.reshape(2, groups, halved * factor, width)


def inverse_columns(stacked, factor):
    halved = factor // 2
    groups, height = (stacked.shape[1], stacked.shape[2])
    blocks = stacked.reshape(2, groups, height, factor, factor)
    section_one = jnp.einsum(
        "pgrjk,pqjn->qgnkr", blocks, complex_table(factor, factor, factor, 1.0), precision=HIGHEST
    )
    section_one = twisted(section_one, factor, 1.0)
    table_real, table_imag = twiddle_table(factor, halved, factor, 1.0)
    last_table = jnp.stack([table_real, -table_imag])
    real_out = jnp.einsum("pgnkr,pkj->grjn", section_one, last_table, precision=HIGHEST)
    scaling = 1.0 / float(factor**4)
    return real_out.reshape(groups, height, halved * factor) * scaling


def body(solution, residual, direction, spectra, basis, slot_channel):
    channel_count = basis.shape[0]
    columns = forward_columns(direction, ROOT)
    swapped = lax.all_to_all(columns, "facet", split_axis=2, concat_axis=3, tiled=True)
    row_spectra = forward_rows(swapped, ROOT)
    weighted = row_spectra * spectra[None]
    inverted = inverse_rows(weighted, ROOT)
    returned = lax.all_to_all(inverted, "facet", split_axis=2, concat_axis=3, tiled=True)
    blurred = inverse_columns(returned, ROOT)
    regrouped = lax.all_to_all(direction, "chan", split_axis=2, concat_axis=0, tiled=True)
    one_hot = (slot_channel[:, None] == jnp.arange(channel_count, dtype=jnp.int32)[None, :]).astype(
        jnp.float32
    )
    loadings = jnp.dot(one_hot, basis, precision=HIGHEST)
    coeffs = jnp.einsum("cq,cij->qij", loadings, regrouped, precision=HIGHEST)
    local_prior = PRIOR_FLOOR * regrouped + jnp.einsum(
        "cq,qij->cij", loadings, coeffs, precision=HIGHEST
    )
    prior_term = lax.all_to_all(local_prior, "chan", split_axis=0, concat_axis=2, tiled=True)
    applied = blurred + prior_term
    norm_now, curvature = lax.psum(
        (jnp.sum(residual * residual), jnp.sum(direction * applied)), ("chan", "facet")
    )
    step_size = norm_now / curvature
    new_solution = solution + step_size * direction
    new_residual = residual - step_size * applied
    norm_next = lax.psum(jnp.sum(new_residual * new_residual), ("chan", "facet"))
    new_direction = new_residual + norm_next / norm_now * direction
    return (new_solution, new_residual, new_direction)


def solution(mesh):
    return jax.shard_map(
        body,
        mesh=mesh,
        in_specs=(
            P("chan", "facet", None),
            P("chan", "facet", None),
            P("chan", "facet", None),
            P("chan", None, "facet"),
            P(),
            P(),
        ),
        out_specs=(P("chan", "facet", None), P("chan", "facet", None), P("chan", "facet", None)),
        check_vma=False,
    )
```

profile of v0, /device:TPU:0, one launch (start us, length us, event | category | flops | bytes accessed | tf_op | source)
XLA Modules:
  0.0 1117.8 jit_solution(16000557213750763182)
XLA Ops:
  25.5 17.9 %convolution_bitcast_fusion.1 = f32[2,1,64,64,512]{4,2,3,0,1:T(8,128)S(1)} fusion(f32[512,32,64]{0,2,1:T(8,128)} %bitcast.178, f32[1,32,64]{2,1,0:T(8,128)S(1)} %get-tuple-element.34, f32[1,32,64]{2,1,0:T(8,128)S(1)} %get-tuple-element.35), kind=kOutput, calls=%fused_computation.36 | convolution fusion | flops 1610616832 | bytes 20987904 | tf_op jit(solution)/shard_map/grjn,qjk->qgknr/dot_general | solution.py:46
  62.4 43.8 %fusion.21 = f32[2,64,64,512]{3,1,2,0:T(8,128)} fusion(f32[2,64,64,512]{3,1,2,0:T(8,128)} %maximum_bitcast_fusion.2, f32[1,2,64,64]{2,3,0,1:T(8,128)S(1)} %get-tuple-element.27, f32[1,2,64,64]{2,3,0,1:T(8,128)S(1)} %get-tuple-element.28), kind=kOutput, calls=%fused_computation.33 | convolution fusion | flops 6442467328 | bytes 33619968 | tf_op jit(solution)/shard_map/pgknr,pqnj->qgjkr/dot_general | solution.py:50
  106.2 15.3 %copy.83 = f32[2,64,64,512]{3,2,1,0:T(8,128)S(1)} copy(f32[2,64,64,512]{3,1,2,0:T(8,128)} %fusion.21) | data formatting | bytes 33554432 | tf_op jit(solution)/shard_map/pgknr,pqnj->qgjkr/dot_general | solution.py:50
  121.5 32.2 %copy.84 = f32[2,1,4096,512]{3,0,1,2:T(2,128)} copy(f32[2,1,4096,512]{3,2,0,1:T(8,128)S(1)} %bitcast.181) | data formatting | bytes 33554432 | tf_op jit(solution)/shard_map/reshape;pgknr,pqnj->qgjkr/transpose | solution.py:56
  160.7 17.8 %copy.90 = f32[64,64,1024]{2,0,1:T(8,128)} copy(f32[64,64,1024]{2,1,0:T(8,128)} %bitcast.185) | data formatting | bytes 33554432 | tf_op jit(solution)/shard_map/mul | solution.py:113
  204.3 139.5 %all-to-all-done = f32[2,1,4096,512]{3,0,1,2:T(2,128)} async-done(((f32[2,1,4096,512]{3,0,1,2:T(2,128)}), f32[2,1,4096,512]{3,0,1,2:T(2,128)}, u32[]{:S(2)}, u32[]{:S(2)}) %all-to-all-start) | async-done | bytes 16777248 | tf_op jit(solution)/shard_map/all_to_all | solution.py:111
  364.3 16.5 %copy.86 = f32[2,1,1024,4,512]{2,4,3,0,1:T(8,128)} copy(f32[2,1,1024,4,512]{4,2,3,0,1:T(8,128)} %bitcast.182) | data formatting | bytes 33554432 | tf_op jit(solution)/shard_map/all_to_all | solution.py:111
  380.8 43.3 %convolution_bitcast_fusion = f32[2,1,64,64,1024]{4,2,3,0,1:T(8,128)} fusion(f32[2,1024,32,64]{1,3,2,0:T(8,128)} %bitcast.179, f32[1,2,32,64]{3,2,1,0:T(8,128)S(1)} %get-tuple-element.33, f32[1,2,32,64]{3,2,1,0:T(8,128)S(1)} %get-tuple-element.32), kind=kOutput, calls=%fused_computation.11 | convolution fusion | flops 6442459136 | bytes 50364416 | tf_op jit(solution)/shard_map/pgcjn,pqjk->qgknc/dot_general | solution.py:63
  424.1 17.6 %multiply_subtract_fusion = (f32[1,1,64,64,1024]{4,2,3,0,1:T(8,128)S(1)}, f32[1,1,64,64,1024]{4,2,3,0,1:T(8,128)}) fusion(f32[2,1,64,64,1024]{4,2,3,0,1:T(8,128)} %convolution_bitcast_fusion, f32[64,64]{0,1:T(8,128)S(1)} %get-tuple-element.36, f32[64,64]{0,1:T(8,128)S(1)} %get-tuple-element.37), kind=kLoop, calls=%fused_computation.28 | loop fusion | flops 25165824 | bytes 67141632 | tf_op jit(solution)/shard_map/sub | solution.py:38
  441.7 19.0 %maximum_bitcast_fusion = f32[2,64,64,1024,1]{3,1,2,0,4:T(8,128)} fusion(f32[1,1,64,64,1024]{4,2,3,0,1:T(8,128)} %get-tuple-element.19, f32[1,1,64,64,1024]{4,2,3,0,1:T(8,128)S(1)} %get-tuple-element.18), kind=kLoop, calls=%fused_computation | loop fusion | flops 8388608 | bytes 67108864 | tf_op jit(solution)/shard_map/reshape.24
  460.8 58.6 %fusion.4 = f32[2,64,64,1024,1]{3,1,4,0,2:T(8,128)} fusion(f32[2,64,64,1024,1]{3,1,2,0,4:T(8,128)} %maximum_bitcast_fusion, f32[1,2,64,64]{2,3,0,1:T(8,128)S(1)} %get-tuple-element.27, f32[1,2,64,64]{2,3,0,1:T(8,128)S(1)} %get-tuple-element.28), kind=kOutput, calls=%fused_computation.7 | convolution fusion | flops 12884918272 | bytes 67174400 | tf_op jit(solution)/shard_map/pgknc,pqnj->qgjkc/dot_general | solution.py:67
  519.3 38.5 %fusion.7 = f32[2,64,64,1024]{3,1,2,0:T(8,128)} fusion(f32[2,64,64,1024,1]{3,1,4,0,2:T(8,128)} %fusion.4, f32[64,64,1024]{2,0,1:T(8,128)} %copy.90, f32[1,2,64,64]{2,3,1,0:T(8,128)S(1)} %copy-done.6, f32[1,2,64,64]{2,3,1,0:T(8,128)S(1)} %copy-done.5), kind=kOutput, calls=%fused_computation.10 | convolution fusion | flops 12893306880 | bytes 83951616 | tf_op jit(solution)/shard_map/pgjkc,pqjn->qgnkc/dot_general | solution.py:80
  557.9 17.7 %subtract_bitcast_fusion = (f32[1,1,64,64,1024]{4,2,3,1,0:T(8,128)S(1)}, f32[1,1,64,64,1024]{4,2,3,1,0:T(8,128)}) fusion(f32[2,64,64,1024]{3,1,2,0:T(8,128)} %fusion.7, f32[64,64]{0,1:T(8,128)S(1)} %fusion.73, f32[64,64]{0,1:T(8,128)S(1)} %get-tuple-element.37), kind=kLoop, calls=%fused_computation.25 | loop fusion | flops 25165824 | bytes 67141632 | tf_op jit(solution)/shard_map/stack | solution.py:37
  575.5 18.8 %maximum_bitcast_fusion.1 = f32[2,64,64,1024]{3,1,2,0:T(8,128)} fusion(f32[1,1,64,64,1024]{4,2,3,1,0:T(8,128)} %get-tuple-element.17, f32[1,1,64,64,1024]{4,2,3,1,0:T(8,128)S(1)} %get-tuple-element.16), kind=kLoop, calls=%fused_computation.1 | loop fusion | flops 8388608 | bytes 67108864 | tf_op jit(solution)/shard_map/reshape.38
  594.3 51.4 %fusion.27 = f32[2,32,64,1024]{3,1,2,0:T(8,128)S(1)} fusion(f32[2,64,64,1024]{3,1,2,0:T(8,128)} %maximum_bitcast_fusion.1, f32[1,2,64,32]{2,3,0,1:T(8,128)S(1)} %copy-done.12, f32[1,2,64,32]{2,3,0,1:T(8,128)S(1)} %copy-done.11), kind=kOutput, calls=%fused_computation.35 | convolution fusion | flops 6442459136 | bytes 50364416 | tf_op jit(solution)/shard_map/pgnkc,pqkj->qgjnc/dot_general | solution.py:84
  645.8 19.4 %copy.93 = f32[2,32,64,1024]{3,2,1,0:T(8,128)} copy(f32[2,32,64,1024]{3,1,2,0:T(8,128)S(1)} %fusion.27) | data formatting | bytes 33554432 | tf_op jit(solution)/shard_map/pgnkc,pqkj->qgjnc/dot_general | solution.py:84
  665.2 28.6 %copy.94 = f32[2,1,2048,1024]{3,0,1,2:T(2,128)} copy(f32[2,1,2048,1024]{3,2,0,1:T(8,128)} %bitcast.183) | data formatting | bytes 33554432 | tf_op jit(solution)/shard_map/reshape;pgnkc,pqkj->qgjnc/transpose | solution.py:90
  715.4 168.4 %all-to-all-done.1 = f32[2,1,2048,1024]{3,0,1,2:T(2,128)} async-done(((f32[2,1,2048,1024]{3,0,1,2:T(2,128)}), f32[2,1,2048,1024]{3,0,1,2:T(2,128)}, u32[]{:S(2)}, u32[]{:S(2)}) %all-to-all-start.1) | async-done | bytes 16777248 | tf_op jit(solution)/shard_map/all_to_all | solution.py:115
  883.8 15.8 %copy.95 = f32[2,1,2048,1024]{3,2,0,1:T(8,128)} copy(f32[2,1,2048,1024]{3,0,1,2:T(2,128)} %all-to-all-done.1) | data formatting | bytes 33554432 | tf_op jit(solution)/shard_map/all_to_all | solution.py:115
  899.6 16.4 %copy.96 = f32[2,1,512,4,1024]{2,4,3,0,1:T(8,128)} copy(f32[2,1,512,4,1024]{4,2,3,0,1:T(8,128)} %bitcast.184) | data formatting | bytes 33554432 | tf_op jit(solution)/shard_map/all_to_all | solution.py:115
  916.1 33.0 %fusion.24 = f32[2,1,64,64,512]{4,2,3,0,1:T(8,128)} fusion(f32[2,512,64,64]{1,3,2,0:T(8,128)} %bitcast.180, f32[1,2,64,64]{2,3,1,0:T(8,128)S(1)} %copy-done.6, f32[1,2,64,64]{2,3,1,0:T(8,128)S(1)} %copy-done.5), kind=kOutput, calls=%fused_computation.34 | convolution fusion | flops 6442467328 | bytes 33619968 | tf_op jit(solution)/shard_map/pgrjk,pqjn->qgnkr/dot_general | solution.py:97
  967.5 18.7 %fusion.33 = f32[1,512,32,64]{1,2,3,0:T(8,128)S(1)} fusion(f32[2,64,64,512]{3,1,2,0:T(8,128)S(1)} %maximum_bitcast_fusion.3, f32[1,64,32]{1,2,0:T(8,128)S(1)} %copy-done.10, f32[1,64,32]{1,2,0:T(8,128)S(1)} %copy-done.8), kind=kOutput, calls=%fused_computation.43 | convolution fusion | flops 1611665408 | bytes 20987904 | tf_op jit(solution)/shard_map/pgnkr,pkj->grjn/dot_general | solution.py:103
  998.1 40.3 %all-reduce = (f32[]{:T(128)}, f32[]{:T(128)}) all-reduce(f32[]{:T(128)} %multiply_reduce_fusion.2, f32[]{:T(128)} %multiply_reduce_fusion.1), channel_id=1, replica_groups=mesh['chan'=8,'facet'=4] {'chan','facet'}, use_global_device_ids=true, to_apply=%region_1.2 | all-reduce | flops 2 | bytes 16 | tf_op jit(solution)/shard_map/psum | solution.py:128
  1048.9 41.4 %psum.23 = f32[]{:T(128)} all-reduce(f32[]{:T(128)} %get-tuple-element.14), channel_id=1, replica_groups=mesh['chan'=8,'facet'=4] {'chan','facet'}, use_global_device_ids=true, to_apply=%region_5.6 | all-reduce | flops 1 | bytes 8 | tf_op jit(solution)/shard_map/psum | solution.py:134
  (70 shorter events, 183.8 us)
Async XLA Ops:
  0.6 178.9 %copy-start = (f32[8,8]{1,0:T(8,128)S(1)}, f32[8,8]{1,0:T(8,128)}, u32[]{:S(2)}) copy-start(f32[8,8]{1,0:T(8,128)} %param.10) | copy-start | bytes 772
  11.5 142.2 %all-to-all-start.2 = ((f32[1,512,2048]{1,0,2:T(1,128)}), f32[1,512,2048]{1,0,2:T(1,128)}, u32[]{:S(2)}, u32[]{:S(2)}) async-start(f32[1,512,2048]{1,0,2:T(1,128)} %copy.101), calls=%async_computation.2 | async-start | bytes 8388608 | tf_op jit(solution)/shard_map/all_to_all | solution.py:117
  153.8 190.0 %all-to-all-start = ((f32[2,1,4096,512]{3,0,1,2:T(2,128)}), f32[2,1,4096,512]{3,0,1,2:T(2,128)}, u32[]{:S(2)}, u32[]{:S(2)}) async-start(f32[2,1,4096,512]{3,0,1,2:T(2,128)} %copy.84), calls=%async_computation | async-start | bytes 33554432 | tf_op jit(solution)/shard_map/all_to_all | solution.py:111
  160.7 18.8 %copy-start.13 = (s32[8]{0:T(128)S(1)}, s32[8]{0:T(128)}, u32[]{:S(2)}) copy-start(s32[8]{0:T(128)} %param.11) | copy-start | bytes 100
  178.7 22.3 %copy-start.7 = (f32[1,64,32]{1,2,0:T(8,128)}, f32[1,64,32]{1,2,0:T(8,128)S(1)}, u32[]{:S(2)}) copy-start(f32[1,64,32]{1,2,0:T(8,128)S(1)} %fusion.88) | copy-start | bytes 24580
  178.9 22.0 %copy-start.9 = (f32[1,64,32]{1,2,0:T(8,128)}, f32[1,64,32]{1,2,0:T(8,128)S(1)}, u32[]{:S(2)}) copy-start(f32[1,64,32]{1,2,0:T(8,128)S(1)} %get-tuple-element.43) | copy-start | bytes 24580
  343.8 350.0 %all-to-all-start.3 = ((f32[8,512,256]{2,1,0:T(8,128)}), f32[8,512,256]{2,1,0:T(8,128)}, u32[]{:S(2)}, u32[]{:S(2)}) async-start(f32[8,512,256]{2,1,0:T(8,128)} %copy.104), calls=%async_computation.3 | async-start | bytes 8388608 | tf_op jit(solution)/shard_map/all_to_all | solution.py:126
  460.8 58.6 %copy-start.5 = (f32[1,2,64,64]{2,3,1,0:T(8,128)S(1)}, f32[1,2,64,64]{2,3,1,0:T(8,128)}, u32[]{:S(2)}) copy-start(f32[1,2,64,64]{2,3,1,0:T(8,128)} %get-tuple-element.26) | copy-start | bytes 98308
  460.8 58.6 %copy-start.6 = (f32[1,2,64,64]{2,3,1,0:T(8,128)S(1)}, f32[1,2,64,64]{2,3,1,0:T(8,128)}, u32[]{:S(2)}) copy-start(f32[1,2,64,64]{2,3,1,0:T(8,128)} %get-tuple-element.29) | copy-start | bytes 98308
  575.5 18.8 %copy-start.11 = (f32[1,2,64,32]{2,3,0,1:T(8,128)S(1)}, f32[1,2,64,32]{2,3,0,1:T(8,128)}, u32[]{:S(2)}) copy-start(f32[1,2,64,32]{2,3,0,1:T(8,128)} %get-tuple-element.30) | copy-start | bytes 49156
  575.5 18.8 %copy-start.12 = (f32[1,2,64,32]{2,3,0,1:T(8,128)S(1)}, f32[1,2,64,32]{2,3,0,1:T(8,128)}, u32[]{:S(2)}) copy-start(f32[1,2,64,32]{2,3,0,1:T(8,128)} %get-tuple-element.31) | copy-start | bytes 49156
  693.8 190.0 %all-to-all-start.1 = ((f32[2,1,2048,1024]{3,0,1,2:T(2,128)}), f32[2,1,2048,1024]{3,0,1,2:T(2,128)}, u32[]{:S(2)}, u32[]{:S(2)}) async-start(f32[2,1,2048,1024]{3,0,1,2:T(2,128)} %copy.94), calls=%async_computation.1 | async-start | bytes 33554432 | tf_op jit(solution)/shard_map/all_to_all | solution.py:115
  960.0 7.4 copy-start.8
  960.0 7.4 copy-start.10
  967.4 23.2 %copy-start.2 = (f32[1,512,2048]{1,2,0:T(8,128)S(1)}, f32[1,512,2048]{1,2,0:T(8,128)}, u32[]{:S(2)}) copy-start(f32[1,512,2048]{1,2,0:T(8,128)} %copy.106) | copy-start | bytes 12582916
  967.5 23.2 %copy-start.3 = (f32[1,512,8,256]{1,3,2,0:T(8,128)S(1)}, f32[1,512,8,256]{1,3,2,0:T(8,128)}, u32[]{:S(2)}) copy-start(f32[1,512,8,256]{1,3,2,0:T(8,128)} %copy.105) | copy-start | bytes 12582916
  988.6 2.0 copy-start.4
  1091.7 25.7 %copy-start.1 = (f32[8,8]{1,0:T(8,128)S(1)}, f32[8,8]{1,0:T(8,128)}, u32[]{:S(2)}) copy-start(f32[8,8]{1,0:T(8,128)} %param.10) | copy-start | bytes 772
where the time goes:
time: 1130 us; the launch traced here: 1120 us
  matrix products  317 us (28%)
  waiting for transfers between devices  308 us (27%)
  local copies, waits for them, and re-layouts  242 us (21%)
  other arithmetic  138 us (12%)
  blocking collectives  81.7 us (7%)
  starting transfers between devices  27.7 us (2%)
    all_to_all x1, waiting for transfers between devices, body(): lax.all_to_all(inverted, 'facet', split_axis=2, concat_axis=3, tiled=True)  168 us
    all_to_all x1, waiting for transfers between devices, body(): lax.all_to_all(columns, 'facet', split_axis=2, concat_axis=3, tiled=True)  140 us
    dot_general x1, matrix products, forward_rows(): jnp.einsum('pgknc,pqnj->qgjkc', section_one, complex_table(factor, factor...  58.6 us
    another operation x4, other arithmetic  57.3 us
    dot_general x1, matrix products, inverse_rows(): jnp.einsum('pgnkc,pqkj->qgjnc', section_one, complex_table(factor, halved...  51.4 us
    unnamed x36, local copies, waits for them, and re-layouts  49.6 us
    dot_general x1, matrix products, forward_columns(): jnp.einsum('pgknr,pqnj->qgjkr', section_one, complex_table(factor, factor...  43.8 us
    dot_general x1, matrix products, forward_rows(): jnp.einsum('pgcjn,pqjk->qgknc', blocks, complex_table(halved, factor, fac...  43.3 us
  transfers between devices with their start and end apart: 4, of which 2 were waited for; matrix products, arithmetic and copies ran while one was open for 48% of the time, Pallas kernels for 0%

commit v1 on v0

--- a/solution.py
+++ b/solution.py
@@ -108,7 +108,18 @@
 def body(solution, residual, direction, spectra, basis, slot_channel):
     channel_count = basis.shape[0]
     columns = forward_columns(direction, ROOT)
-    swapped = lax.all_to_all(columns, "facet", split_axis=2, concat_axis=3, tiled=True)
+    ways, here = (lax.axis_size("facet"), lax.axis_index("facet"))
+    width_2 = columns.shape[2] // ways
+    shape = list(columns.shape)
+    shape[2] = width_2
+    height_2 = shape[3]
+    shape[3] = height_2 * ways
+    swapped = jnp.zeros(shape, columns.dtype)
+    for mask in range(ways):
+        part = lax.dynamic_slice_in_dim(columns, (here ^ mask) * width_2, width_2, axis=2)
+        if mask:
+            part = lax.ppermute(part, "facet", [(d, d ^ mask) for d in range(ways)])
+        swapped = lax.dynamic_update_slice_in_dim(swapped, part, (here ^ mask) * height_2, axis=3)
     row_spectra = forward_rows(swapped, ROOT)
     weighted = row_spectra * spectra[None]
     inverted = inverse_rows(weighted, ROOT)

time: 1130 us -> 1080 us (0.956)
  waiting for transfers between devices: 308 us -> 278 us
    all_to_all x1 -> x0, waiting for transfers between devices: 140 us -> none  [body(): lax.all_to_all(columns, 'facet', split_axis=2, concat_axis=3, tiled=True)]
    ppermute x0 -> x3, waiting for transfers between devices: none -> 109 us  [body(): part = lax.ppermute(part, 'facet', [(d, d ^ mask) for d in range(ways)])]
    transpose x1 -> x0, local copies, waits for them, and re-layouts: 32.2 us -> none  [forward_columns(): return second.reshape(2, groups, factor * factor, height)]
    all_to_all x2 -> x0, local copies, waits for them, and re-layouts: 30.6 us -> none  [body(): lax.all_to_all(columns, 'facet', split_axis=2, concat_axis=3, tiled=True)]
    dynamic_slice x0 -> x2, local copies, waits for them, and re-layouts: none -> 17.8 us  [body(): lax.dynamic_slice_in_dim(columns, (here ^ mask) * width_2, width_2, axis=2)]
    dynamic_update_slice x0 -> x4, local copies, waits for them, and re-layouts: none -> 16.5 us  [body(): lax.dynamic_update_slice_in_dim(swapped, part, (here ^ mask) * height_2,...]
    ppermute x0 -> x3, local copies, waits for them, and re-layouts: none -> 16.2 us  [body(): part = lax.ppermute(part, 'facet', [(d, d ^ mask) for d in range(ways)])]
    unnamed x36 -> x38, local copies, waits for them, and re-layouts: 49.6 us -> 49.7 us
  transfers between devices with their start and end apart: 4 -> 6, of which waited for: 2 -> 3; matrix products, arithmetic and copies ran while one was open for 48% -> 38% of each run, Pallas kernels for 0% -> 0%
where the time goes in v1:
time: 1080 us; the launch traced here: 1070 us
  matrix products  307 us (28%)
  waiting for transfers between devices  278 us (26%)
  local copies, waits for them, and re-layouts  240 us (22%)
  other arithmetic  138 us (13%)
  blocking collectives  81.7 us (8%)
  starting transfers between devices  22 us (2%)
    all_to_all x1, waiting for transfers between devices, body(): lax.all_to_all(inverted, 'facet', split_axis=2, concat_axis=3, tiled=True)  168 us
    ppermute x3, waiting for transfers between devices, body(): part = lax.ppermute(part, 'facet', [(d, d ^ mask) for d in range(ways)])  109 us
    dot_general x1, matrix products, forward_rows(): jnp.einsum('pgknc,pqnj->qgjkc', section_one, complex_table(factor, factor...  58.8 us
    another operation x4, other arithmetic  57.6 us
    dot_general x1, matrix products, inverse_rows(): jnp.einsum('pgnkc,pqkj->qgjnc', section_one, complex_table(factor, halved...  51.4 us
    unnamed x38, local copies, waits for them, and re-layouts  49.7 us
    dot_general x1, matrix products, forward_rows(): jnp.einsum('pgcjn,pqjk->qgknc', blocks, complex_table(halved, factor, fac...  43.6 us
    psum x1, blocking collectives, body(): lax.psum(jnp.sum(new_residual * new_residual), ('chan', 'facet'))  41.4 us
  transfers between devices with their start and end apart: 6, of which 3 were waited for; matrix products, arithmetic and copies ran while one was open for 38% of the time, Pallas kernels for 0%

profile of v1, /device:TPU:0, one launch (start us, length us, event | category | flops | bytes accessed | tf_op | source)
XLA Modules:
  0.0 1070.5 jit_solution(7363310896771513146)
XLA Ops:
  6.7 17.9 %convolution_bitcast_fusion.1 = f32[2,1,64,64,512]{4,2,3,0,1:T(8,128)S(1)} fusion(f32[512,32,64]{0,2,1:T(8,128)} %bitcast.175, f32[1,32,64]{2,1,0:T(8,128)S(1)} %get-tuple-element.38, f32[1,32,64]{2,1,0:T(8,128)S(1)} %get-tuple-element.39), kind=kOutput, calls=%fused_computation.36 | convolution fusion | flops 1610616832 | bytes 20987904 | tf_op jit(solution)/shard_map/grjn,qjk->qgknr/dot_general | solution.py:46
  44.2 33.2 %fusion.21 = f32[2,64,64,512]{3,1,2,0:T(8,128)} fusion(f32[2,64,64,512]{3,1,2,0:T(8,128)} %maximum_bitcast_fusion.2, f32[1,2,64,64]{2,3,0,1:T(8,128)S(1)} %get-tuple-element.31, f32[1,2,64,64]{2,3,0,1:T(8,128)S(1)} %get-tuple-element.32), kind=kOutput, calls=%fused_computation.33 | convolution fusion | flops 6442467328 | bytes 33619968 | tf_op jit(solution)/shard_map/pgknr,pqnj->qgjkr/dot_general | solution.py:50
  77.4 17.7 %copy.89 = f32[2,64,64,512]{3,2,1,0:T(8,128)} copy(f32[2,64,64,512]{3,1,2,0:T(8,128)} %fusion.21) | data formatting | bytes 33554432 | tf_op jit(solution)/shard_map/pgknr,pqnj->qgjkr/dot_general | solution.py:50
  95.2 12.4 %constant_dynamic-slice_fusion = (f32[2,1,1024,512]{3,2,0,1:T(8,128)}, f32[2,1,1024,512]{3,2,0,1:T(8,128)}, f32[2,1,1024,512]{3,2,0,1:T(8,128)}, f32[2,1,1024,512]{3,2,0,1:T(8,128)}) fusion(f32[2,1,4096,512]{3,2,0,1:T(8,128)} %bitcast.176, s32[]{:T(128)S(6)} %select_n.196, s32[]{:T(128)S(6)} %select_n.194, s32[]{:T(128)S(6)} %select_n.192, s32[]{:T(128)S(6)} %select_n.190), kind=kLoop, calls=%fused_computation.135 | loop fusion | bytes 33554448 | tf_op jit(solution)/shard_map/dynamic_slice | solution.py:119
  133.0 17.7 %copy.97 = f32[64,64,1024]{2,0,1:T(8,128)} copy(f32[64,64,1024]{2,1,0:T(8,128)} %bitcast.180) | data formatting | bytes 33554432 | tf_op jit(solution)/shard_map/mul | solution.py:124
  167.6 34.7 %collective-permute-done.1 = f32[2,1,1024,512]{3,2,0,1:T(8,128)} collective-permute-done((f32[2,1,1024,512]{3,2,0,1:T(8,128)}, f32[2,1,1024,512]{3,2,0,1:T(8,128)}, u32[]{:S(2)}, u32[]{:S(2)}) %collective-permute-start.1) | collective-permute-done | bytes 4194336 | tf_op jit(solution)/shard_map/ppermute | solution.py:121
  217.2 74.5 %collective-permute-done.2 = f32[2,1,1024,512]{3,2,0,1:T(8,128)} collective-permute-done((f32[2,1,1024,512]{3,2,0,1:T(8,128)}, f32[2,1,1024,512]{3,2,0,1:T(8,128)}, u32[]{:S(2)}, u32[]{:S(2)}) %collective-permute-start.2) | collective-permute-done | bytes 4194336 | tf_op jit(solution)/shard_map/ppermute | solution.py:121
  301.9 43.6 %convolution_bitcast_fusion = f32[2,1,64,64,1024]{4,2,3,0,1:T(8,128)} fusion(f32[2,1024,32,64]{1,3,2,0:T(8,128)} %bitcast.30, f32[1,2,32,64]{3,2,1,0:T(8,128)S(1)} %get-tuple-element.37, f32[1,2,32,64]{3,2,1,0:T(8,128)S(1)} %get-tuple-element.36), kind=kOutput, calls=%fused_computation.11 | convolution fusion | flops 6442459136 | bytes 50364416 | tf_op jit(solution)/shard_map/pgcjn,pqjk->qgknc/dot_general | solution.py:63
  345.4 17.7 %multiply_subtract_fusion = (f32[1,1,64,64,1024]{4,2,3,0,1:T(8,128)S(1)}, f32[1,1,64,64,1024]{4,2,3,0,1:T(8,128)}) fusion(f32[2,1,64,64,1024]{4,2,3,0,1:T(8,128)} %convolution_bitcast_fusion, f32[64,64]{0,1:T(8,128)S(1)} %get-tuple-element.40, f32[64,64]{0,1:T(8,128)S(1)} %get-tuple-element.41), kind=kLoop, calls=%fused_computation.28 | loop fusion | flops 25165824 | bytes 67141632 | tf_op jit(solution)/shard_map/sub | solution.py:38
  363.2 19.1 %maximum_bitcast_fusion = f32[2,64,64,1024,1]{3,1,2,0,4:T(8,128)} fusion(f32[1,1,64,64,1024]{4,2,3,0,1:T(8,128)} %get-tuple-element.19, f32[1,1,64,64,1024]{4,2,3,0,1:T(8,128)S(1)} %get-tuple-element.18), kind=kLoop, calls=%fused_computation | loop fusion | flops 8388608 | bytes 67108864 | tf_op jit(solution)/shard_map/reshape.23
  382.2 58.8 %fusion.4 = f32[2,64,64,1024,1]{3,1,4,0,2:T(8,128)} fusion(f32[2,64,64,1024,1]{3,1,2,0,4:T(8,128)} %maximum_bitcast_fusion, f32[1,2,64,64]{2,3,0,1:T(8,128)S(1)} %get-tuple-element.31, f32[1,2,64,64]{2,3,0,1:T(8,128)S(1)} %get-tuple-element.32), kind=kOutput, calls=%fused_computation.7 | convolution fusion | flops 12884918272 | bytes 67174400 | tf_op jit(solution)/shard_map/pgknc,pqnj->qgjkc/dot_general | solution.py:67
  471.4 38.6 %fusion.7 = f32[2,64,64,1024]{3,1,2,0:T(8,128)} fusion(f32[2,64,64,1024,1]{3,1,4,0,2:T(8,128)} %fusion.4, f32[64,64,1024]{2,0,1:T(8,128)} %copy.97, f32[1,2,64,64]{2,3,1,0:T(8,128)S(1)} %copy-done.7, f32[1,2,64,64]{2,3,1,0:T(8,128)S(1)} %copy-done.6), kind=kOutput, calls=%fused_computation.10 | convolution fusion | flops 12893306880 | bytes 83951616 | tf_op jit(solution)/shard_map/pgjkc,pqjn->qgnkc/dot_general | solution.py:80
  510.0 17.6 %subtract_bitcast_fusion = (f32[1,1,64,64,1024]{4,2,3,1,0:T(8,128)S(1)}, f32[1,1,64,64,1024]{4,2,3,1,0:T(8,128)}) fusion(f32[2,64,64,1024]{3,1,2,0:T(8,128)} %fusion.7, f32[64,64]{0,1:T(8,128)S(1)} %fusion.73, f32[64,64]{0,1:T(8,128)S(1)} %get-tuple-element.41), kind=kLoop, calls=%fused_computation.25 | loop fusion | flops 25165824 | bytes 67141632 | tf_op jit(solution)/shard_map/stack | solution.py:37
  527.6 19.1 %maximum_bitcast_fusion.1 = f32[2,64,64,1024]{3,1,2,0:T(8,128)} fusion(f32[1,1,64,64,1024]{4,2,3,1,0:T(8,128)} %get-tuple-element.17, f32[1,1,64,64,1024]{4,2,3,1,0:T(8,128)S(1)} %get-tuple-element.16), kind=kLoop, calls=%fused_computation.1 | loop fusion | flops 8388608 | bytes 67108864 | tf_op jit(solution)/shard_map/reshape.37
  546.6 51.4 %fusion.27 = f32[2,32,64,1024]{3,1,2,0:T(8,128)S(1)} fusion(f32[2,64,64,1024]{3,1,2,0:T(8,128)} %maximum_bitcast_fusion.1, f32[1,2,64,32]{2,3,0,1:T(8,128)S(1)} %copy-done.13, f32[1,2,64,32]{2,3,0,1:T(8,128)S(1)} %copy-done.12), kind=kOutput, calls=%fused_computation.35 | convolution fusion | flops 6442459136 | bytes 50364416 | tf_op jit(solution)/shard_map/pgnkc,pqkj->qgjnc/dot_general | solution.py:84
  598.1 19.4 %copy.100 = f32[2,32,64,1024]{3,2,1,0:T(8,128)} copy(f32[2,32,64,1024]{3,1,2,0:T(8,128)S(1)} %fusion.27) | data formatting | bytes 33554432 | tf_op jit(solution)/shard_map/pgnkc,pqkj->qgjnc/dot_general | solution.py:84
  617.5 28.6 %copy.101 = f32[2,1,2048,1024]{3,0,1,2:T(2,128)} copy(f32[2,1,2048,1024]{3,2,0,1:T(8,128)} %bitcast.178) | data formatting | bytes 33554432 | tf_op jit(solution)/shard_map/reshape;pgnkc,pqkj->qgjnc/transpose | solution.py:90
  667.7 168.4 %all-to-all-done = f32[2,1,2048,1024]{3,0,1,2:T(2,128)} async-done(((f32[2,1,2048,1024]{3,0,1,2:T(2,128)}), f32[2,1,2048,1024]{3,0,1,2:T(2,128)}, u32[]{:S(2)}, u32[]{:S(2)}) %all-to-all-start) | async-done | bytes 16777248 | tf_op jit(solution)/shard_map/all_to_all | solution.py:126
  836.1 15.8 %copy.102 = f32[2,1,2048,1024]{3,2,0,1:T(8,128)} copy(f32[2,1,2048,1024]{3,0,1,2:T(2,128)} %all-to-all-done) | data formatting | bytes 33554432 | tf_op jit(solution)/shard_map/all_to_all | solution.py:126
  852.0 16.5 %copy.103 = f32[2,1,512,4,1024]{2,4,3,0,1:T(8,128)} copy(f32[2,1,512,4,1024]{4,2,3,0,1:T(8,128)} %bitcast.179) | data formatting | bytes 33554432 | tf_op jit(solution)/shard_map/all_to_all | solution.py:126
  868.4 33.0 %fusion.24 = f32[2,1,64,64,512]{4,2,3,0,1:T(8,128)} fusion(f32[2,512,64,64]{1,3,2,0:T(8,128)} %bitcast.177, f32[1,2,64,64]{2,3,1,0:T(8,128)S(1)} %copy-done.7, f32[1,2,64,64]{2,3,1,0:T(8,128)S(1)} %copy-done.6), kind=kOutput, calls=%fused_computation.34 | convolution fusion | flops 6442467328 | bytes 33619968 | tf_op jit(solution)/shard_map/pgrjk,pqjn->qgnkr/dot_general | solution.py:97
  919.8 18.7 %fusion.33 = f32[1,512,32,64]{1,2,3,0:T(8,128)S(1)} fusion(f32[2,64,64,512]{3,1,2,0:T(8,128)S(1)} %maximum_bitcast_fusion.3, f32[1,64,32]{1,2,0:T(8,128)S(1)} %copy-done.11, f32[1,64,32]{1,2,0:T(8,128)S(1)} %copy-done.9), kind=kOutput, calls=%fused_computation.43 | convolution fusion | flops 1611665408 | bytes 20987904 | tf_op jit(solution)/shard_map/pgnkr,pkj->grjn/dot_general | solution.py:103
  950.6 40.3 %all-reduce = (f32[]{:T(128)}, f32[]{:T(128)}) all-reduce(f32[]{:T(128)} %multiply_reduce_fusion.2, f32[]{:T(128)} %multiply_reduce_fusion.1), channel_id=1, replica_groups=mesh['chan'=8,'facet'=4] {'chan','facet'}, use_global_device_ids=true, to_apply=%region_1.2 | all-reduce | flops 2 | bytes 16 | tf_op jit(solution)/shard_map/psum | solution.py:139
  1001.6 41.4 %psum.23 = f32[]{:T(128)} all-reduce(f32[]{:T(128)} %get-tuple-element.14), channel_id=1, replica_groups=mesh['chan'=8,'facet'=4] {'chan','facet'}, use_global_device_ids=true, to_apply=%region_5.6 | all-reduce | flops 1 | bytes 8 | tf_op jit(solution)/shard_map/psum | solution.py:145
  (83 shorter events, 210.1 us)
Async XLA Ops:
  0.6 151.2 %copy-start = (f32[8,8]{1,0:T(8,128)S(1)}, f32[8,8]{1,0:T(8,128)}, u32[]{:S(2)}) copy-start(f32[8,8]{1,0:T(8,128)} %param.10) | copy-start | bytes 772
  107.6 54.6 %collective-permute-start = (f32[2,1,1024,512]{3,2,0,1:T(8,128)}, f32[2,1,1024,512]{3,2,0,1:T(8,128)}, u32[]{:S(2)}, u32[]{:S(2)}) collective-permute-start(f32[2,1,1024,512]{3,2,0,1:T(8,128)} %get-tuple-element.26), channel_id=1, source_target_pairs={{0,1},{1,0},{2,3},{3,2},{4,5},{5,4},{6,7},{7,6},{8,9},{9,8},{10,11... | collective-permute-start | bytes 12582920 | tf_op jit(solution)/shard_map/ppermute | solution.py:121
  108.1 94.3 %collective-permute-start.1 = (f32[2,1,1024,512]{3,2,0,1:T(8,128)}, f32[2,1,1024,512]{3,2,0,1:T(8,128)}, u32[]{:S(2)}, u32[]{:S(2)}) collective-permute-start(f32[2,1,1024,512]{3,2,0,1:T(8,128)} %get-tuple-element.25), channel_id=1, source_target_pairs={{0,2},{1,3},{2,0},{3,1},{4,6},{5,7},{6,4},{7,5},{8,10},{9,11},{10,... | collective-permute-start | bytes 12582920 | tf_op jit(solution)/shard_map/ppermute | solution.py:121
  110.6 181.1 %collective-permute-start.2 = (f32[2,1,1024,512]{3,2,0,1:T(8,128)}, f32[2,1,1024,512]{3,2,0,1:T(8,128)}, u32[]{:S(2)}, u32[]{:S(2)}) collective-permute-start(f32[2,1,1024,512]{3,2,0,1:T(8,128)} %get-tuple-element.24), channel_id=1, source_target_pairs={{0,3},{1,2},{2,1},{3,0},{4,7},{5,6},{6,5},{7,4},{8,11},{9,10},{10,... | collective-permute-start | bytes 12582920 | tf_op jit(solution)/shard_map/ppermute | solution.py:121
  121.5 319.5 %all-to-all-start.1 = ((f32[1,512,2048]{1,0,2:T(1,128)}), f32[1,512,2048]{1,0,2:T(1,128)}, u32[]{:S(2)}, u32[]{:S(2)}) async-start(f32[1,512,2048]{1,0,2:T(1,128)} %copy.108), calls=%async_computation.1 | async-start | bytes 8388608 | tf_op jit(solution)/shard_map/all_to_all | solution.py:128
  133.0 18.8 %copy-start.14 = (s32[8]{0:T(128)S(1)}, s32[8]{0:T(128)}, u32[]{:S(2)}) copy-start(s32[8]{0:T(128)} %param.11) | copy-start | bytes 100
  150.7 9.2 copy-start.5
  150.9 11.3 %copy-start.8 = (f32[1,64,32]{1,2,0:T(8,128)}, f32[1,64,32]{1,2,0:T(8,128)S(1)}, u32[]{:S(2)}) copy-start(f32[1,64,32]{1,2,0:T(8,128)S(1)} %fusion.88) | copy-start | bytes 24580
  151.1 11.1 %copy-start.10 = (f32[1,64,32]{1,2,0:T(8,128)}, f32[1,64,32]{1,2,0:T(8,128)S(1)}, u32[]{:S(2)}) copy-start(f32[1,64,32]{1,2,0:T(8,128)S(1)} %get-tuple-element.47) | copy-start | bytes 24580
  456.5 14.8 %copy-start.6 = (f32[1,2,64,64]{2,3,1,0:T(8,128)S(1)}, f32[1,2,64,64]{2,3,1,0:T(8,128)}, u32[]{:S(2)}) copy-start(f32[1,2,64,64]{2,3,1,0:T(8,128)} %get-tuple-element.30) | copy-start | bytes 98308
  456.5 14.8 %copy-start.7 = (f32[1,2,64,64]{2,3,1,0:T(8,128)S(1)}, f32[1,2,64,64]{2,3,1,0:T(8,128)}, u32[]{:S(2)}) copy-start(f32[1,2,64,64]{2,3,1,0:T(8,128)} %get-tuple-element.33) | copy-start | bytes 98308
  465.5 180.6 %all-to-all-start.2 = ((f32[8,512,256]{2,1,0:T(8,128)}), f32[8,512,256]{2,1,0:T(8,128)}, u32[]{:S(2)}, u32[]{:S(2)}) async-start(f32[8,512,256]{2,1,0:T(8,128)} %copy.111), calls=%async_computation.2 | async-start | bytes 8388608 | tf_op jit(solution)/shard_map/all_to_all | solution.py:137
  527.6 19.1 %copy-start.12 = (f32[1,2,64,32]{2,3,0,1:T(8,128)S(1)}, f32[1,2,64,32]{2,3,0,1:T(8,128)}, u32[]{:S(2)}) copy-start(f32[1,2,64,32]{2,3,0,1:T(8,128)} %get-tuple-element.34) | copy-start | bytes 49156
  527.6 19.1 %copy-start.13 = (f32[1,2,64,32]{2,3,0,1:T(8,128)S(1)}, f32[1,2,64,32]{2,3,0,1:T(8,128)}, u32[]{:S(2)}) copy-start(f32[1,2,64,32]{2,3,0,1:T(8,128)} %get-tuple-element.35) | copy-start | bytes 49156
  646.1 190.0 %all-to-all-start = ((f32[2,1,2048,1024]{3,0,1,2:T(2,128)}), f32[2,1,2048,1024]{3,0,1,2:T(2,128)}, u32[]{:S(2)}, u32[]{:S(2)}) async-start(f32[2,1,2048,1024]{3,0,1,2:T(2,128)} %copy.101), calls=%async_computation | async-start | bytes 33554432 | tf_op jit(solution)/shard_map/all_to_all | solution.py:126
  912.4 7.4 copy-start.9
  912.4 7.4 copy-start.11
  919.8 23.2 %copy-start.2 = (f32[1,512,2048]{1,2,0:T(8,128)S(1)}, f32[1,512,2048]{1,2,0:T(8,128)}, u32[]{:S(2)}) copy-start(f32[1,512,2048]{1,2,0:T(8,128)} %copy.113) | copy-start | bytes 12582916
  919.8 23.2 %copy-start.3 = (f32[1,512,8,256]{1,3,2,0:T(8,128)S(1)}, f32[1,512,8,256]{1,3,2,0:T(8,128)}, u32[]{:S(2)}) copy-start(f32[1,512,8,256]{1,3,2,0:T(8,128)} %copy.112) | copy-start | bytes 12582916
  941.0 2.0 copy-start.4
  1044.4 25.7 %copy-start.1 = (f32[8,8]{1,0:T(8,128)S(1)}, f32[8,8]{1,0:T(8,128)}, u32[]{:S(2)}) copy-start(f32[8,8]{1,0:T(8,128)} %param.10) | copy-start | bytes 772
